TPU v7x, 32 devices: a whole 2x2x4 slice. The times are simulated.
32 devices in a mesh: groups: 2 (over y), cls: 4 (over z), img: 4 (over x, core).
Axes of the slice: x: 2, y: 2, z: 4, core: 2. Of those that a mesh axis runs over, the one named last changes fastest.
Arguments:
- particles: bfloat16 [512, 2, 4608], P(('groups', 'img', 'cls')), parts along dimension 0, may hold values from -30 to 30
- classes: bfloat16 [256, 2, 4608], P(('groups', 'cls')), parts along dimension 0, may hold values from -4 to 4
- ctf: float32 [128, 4608], P('groups'), parts along dimension 0, may hold values from 0.1 to 1
- noise_weight: float32 [9216], P('groups'), parts along dimension 0, may hold values from 0.01 to 0.1
- group_ids: int32 [512], P(('groups', 'img', 'cls')), parts along dimension 0, may hold values from 0 to 63
- shifts: int32 [48, 2], P('groups'), parts along dimension 0, may hold values from -6 to 6
Outputs:
- log_resp: float32 [512, 128], P(('groups', 'img'), 'cls'), parts along dimension 0
- averages: float32 [256, 2, 4608], P(('groups', 'cls'), None, 'img'), parts along dimension 0
There are 2 independent parts, one for each index of `groups`. A program takes and returns all parts, laid end to end along the dimension named above; each array names one. Nothing has to cross between parts.
All inputs are finite; a program needn't handle non-finite values.
Results may differ from a plain program's by a relative error of at most 0.012.
The roundings to bfloat16 on the way count: a program that leaves them out, or rounds other values in their place, can miss the bound.
Values may be sent and summed in bfloat16 or wider, within the bound.
A program may use at most 128 MiB of HBM per device.

v0:
```python
import jax
import jax.numpy as jnp
from jax import lax
from jax.sharding import PartitionSpec as P

BOX = 128


prior_precision = 0.02


def phase_tables(shifts, freq):
    index = jnp.arange(freq)
    along_y = (index // BOX).astype(jnp.float32)
    along_x = (index % BOX - BOX // 2).astype(jnp.float32)
    angle = (
        2.0
        * jnp.pi
        / BOX
        * (
            shifts[:, 0:1].astype(jnp.float32) * along_x[None, :]
            + shifts[:, 1:2].astype(jnp.float32) * along_y[None, :]
        )
    )
    return (jnp.cos(angle), jnp.sin(angle))


def local(particles, classes, ctf, noise_weight, group_ids, shifts):
    part_rows = particles.shape[0]
    freq = particles.shape[2]
    cls_rows = classes.shape[0]
    poses = shifts.shape[0]
    groups = ctf.shape[0]
    total_rows = part_rows * lax.axis_size("cls")
    cos_t, sin_t = phase_tables(shifts, freq)
    real_part = classes[:, 0, :].astype(jnp.float32)
    imag_part = classes[:, 1, :].astype(jnp.float32)
    temp_re = real_part[None] * cos_t[:, None, :] - imag_part[None] * sin_t[:, None, :]
    temp_im = real_part[None] * sin_t[:, None, :] + imag_part[None] * cos_t[:, None, :]
    templates = (
        jnp.stack([temp_re, temp_im], axis=2)
        .astype(jnp.bfloat16)
        .reshape(poses * cls_rows, 2 * freq)
    )
    marks_local = (group_ids[:, None] == jnp.arange(groups)[None, :]).astype(jnp.float32)
    selected = jnp.dot(marks_local, ctf, precision=lax.Precision.HIGHEST)
    weighted = (
        particles.astype(jnp.float32) * (selected * noise_weight[None, :])[:, None, :]
    ).astype(jnp.bfloat16)
    weighted = weighted.reshape(part_rows, 2 * freq)
    marks_low = marks_local.astype(jnp.bfloat16)
    ctf_weight = ctf * ctf * noise_weight[None, :]
    power = jnp.dot(
        ctf_weight,
        (real_part * real_part + imag_part * imag_part).T,
        precision=lax.Precision.HIGHEST,
    )
    gathered, marks_all = (
        lax.all_gather(weighted, "cls", axis=0, tiled=True),
        lax.all_gather(marks_low, "cls", axis=0, tiled=True),
    )
    cross = lax.dot_general(
        gathered, templates, (((1,), (1,)), ((), ())), preferred_element_type=jnp.float32
    )
    penalty = jnp.dot(marks_all.astype(jnp.float32), power, precision=lax.Precision.HIGHEST)
    scores = cross.reshape(gathered.shape[0], poses, cls_rows) - 0.5 * penalty[:, None, :]
    local_peak = jnp.max(scores, axis=(1, 2))
    peak = lax.pmax(local_peak, "cls")
    total = lax.psum(jnp.sum(jnp.exp(scores - peak[:, None, None]), axis=(1, 2)), "cls")
    log_norm = peak + jnp.log(total)
    pose_peak = jnp.max(scores, axis=1)
    log_resp = (
        pose_peak
        + jnp.log(jnp.sum(jnp.exp(scores - pose_peak[:, None, :]), axis=1))
        - log_norm[:, None]
    )
    rho = jnp.exp(scores - log_norm[:, None, None])
    rho_low = rho.astype(jnp.bfloat16).reshape(total_rows, poses * cls_rows)
    pose_total = jnp.sum(rho, axis=1)
    sums = lax.dot_general(
        rho_low, gathered, (((0,), (0,)), ((), ())), preferred_element_type=jnp.float32
    )
    mass_table = jnp.dot(
        pose_total.T, marks_all.astype(jnp.float32), precision=lax.Precision.HIGHEST
    )
    sums = sums.reshape(poses, cls_rows, 2, freq)
    cos_b = cos_t[:, None, :]
    sin_b = sin_t[:, None, :]
    numer_re = jnp.sum(sums[:, :, 0, :] * cos_b + sums[:, :, 1, :] * sin_b, axis=0)
    numer_im = jnp.sum(sums[:, :, 1, :] * cos_b - sums[:, :, 0, :] * sin_b, axis=0)
    numer = jnp.stack([numer_re, numer_im], axis=1)
    denom = jnp.dot(mass_table, ctf_weight, precision=lax.Precision.HIGHEST)
    numer_part, denom_part = (
        lax.psum_scatter(numer, "img", scatter_dimension=2, tiled=True),
        lax.psum_scatter(denom, "img", scatter_dimension=1, tiled=True),
    )
    averages = numer_part / (denom_part[:, None, :] + prior_precision)
    return (log_resp, averages)


def solution(mesh):
    placed = (
        P(("groups", "img", "cls"), None, None),
        P(("groups", "cls"), None, None),
        P("groups", None),
        P("groups"),
        P(("groups", "img", "cls")),
        P("groups", None),
    )
    return jax.shard_map(
        local,
        mesh=mesh,
        in_specs=placed,
        out_specs=(P(("groups", "img"), "cls"), P(("groups", "cls"), None, "img")),
        check_vma=False,
    )
```

profile of v0, /device:TPU:1, one launch (start us, length us, event | category | flops | bytes accessed | tf_op | source)
XLA Modules:
  0.0 219.9 jit_solution(17909339871494409727)
XLA Ops:
  7.2 1.8 convolution_multiply_fusion
  9.0 1.3 multiply_convert_fusion
  10.3 0.7 copy.26
  11.0 0.0 reduce-scatter.5.cloned.1.call-start
  11.1 2.4 %fusion.34 = (bf16[32,1,4608]{2,1,0:T(2,128)(2,1)S(1)}, bf16[32,1,4608]{2,1,0:T(2,128)(2,1)S(1)}) fusion(bf16[32,2,4608]{2,1,0:T(2,128)(2,1)} %param.7), kind=kLoop, calls=%fused_computation.61 | loop fusion | bytes 1179648 | tf_op jit(solution)/shard_map/slice | solution.py:36
  13.5 0.8 convert_bitcast_fusion.1
  14.3 0.1 fusion.18
  14.3 1.6 fusion.15
  16.0 30.8 %subtract_convert_fusion = (bf16[24,32,1,4608]{3,2,1,0:T(2,128)(2,1)S(1)}, bf16[24,32,1,4608]{3,2,1,0:T(2,128)(2,1)}) fusion(f32[24,4608]{1,0:T(8,128)S(1)} %get-tuple-element.17, f32[32,4608]{1,0:T(8,128)S(1)} %get-tuple-element.22, f32[24,4608]{1,0:T(8,128)S(1)} %get-tuple-element.16, f32[32,4608]{1,0:T(8,128)S(1)} %get-tuple-element.23), kind=kLoop, calls=%fused_computation.6 | loop fusion | flops 28311552 | bytes 16220160 | tf_op jit(solution)/shard_map/convert.2
  46.8 34.8 %pad_maximum_fusion = bf16[24,32,2,4608]{3,2,1,0:T(2,128)(2,1)} fusion(bf16[24,32,1,4608]{3,2,1,0:T(2,128)(2,1)} %get-tuple-element.13, bf16[24,32,1,4608]{3,2,1,0:T(2,128)(2,1)S(1)} %get-tuple-element.12), kind=kLoop, calls=%fused_computation.2 | loop fusion | flops 28311552 | bytes 28311552 | tf_op jit(solution)/shard_map/stack | solution.py:41
  81.6 22.7 %convert_element_type.73 = bf16[24,32,9216]{2,1,0:T(8,128)(2,1)} reshape(bf16[24,32,2,4608]{3,2,1,0:T(2,128)(2,1)} %pad_maximum_fusion) | data formatting | bytes 28311552 | tf_op jit(solution)/shard_map/convert_element_type | solution.py:42
  104.3 0.1 convert_convert_fusion
  104.4 11.3 %all_gather.7 = bf16[64,64]{1,0:T(8,128)(2,1)S(1)} all-gather(bf16[16,64]{1,0:T(8,128)(2,1)S(1)} %convert_convert_fusion), channel_id=1, replica_groups=mesh['groups'=2,'cls'=4,'img'=4] {'cls'}, dimensions={0}, use_global_device_ids=true | all-gather | bytes 10240 | tf_op jit(solution)/shard_map/all_gather | solution.py:60
  115.7 1.2 fusion.8
  116.9 0.1 convolution_multiply_fusion.1
  117.0 0.0 all-gather.2.cloned.1.call-done
  117.1 7.5 %fusion.35 = (f32[64]{0:T(128)S(1)}, f32[64,24,32]{0,2,1:T(8,128)S(1)}) fusion(f32[64,32]{0,1:T(8,128)S(1)} %convolution_multiply_fusion.1, bf16[24,32,9216]{2,1,0:T(8,128)(2,1)} %convert_element_type.73, bf16[64,9216]{1,0:T(8,128)(2,1)} %all-gather.2.cloned.1.call-done), kind=kOutput, calls=%fused_computation.62 | convolution fusion | flops 906067904 | bytes 15540480 | tf_op jit(solution)/shard_map/dot_general | solution.py:62
  124.6 9.9 %pmax.7 = f32[64]{0:T(128)S(1)} all-reduce(f32[64]{0:T(128)S(1)} %get-tuple-element.20), channel_id=1, replica_groups=mesh['groups'=2,'cls'=4,'img'=4] {'cls'}, use_global_device_ids=true, to_apply=%region_3.4 | all-reduce | flops 64 | bytes 512 | tf_op jit(solution)/shard_map/pmax | solution.py:68
  134.5 0.1 exponential_reduce_fusion
  134.6 6.8 %psum.7 = f32[64]{0:T(128)S(1)} all-reduce(f32[64]{0:T(128)S(1)} %get-tuple-element.10), channel_id=1, replica_groups=mesh['groups'=2,'cls'=4,'img'=4] {'cls'}, use_global_device_ids=true, to_apply=%region_5.6 | all-reduce | flops 64 | bytes 512 | tf_op jit(solution)/shard_map/psum | solution.py:69
  141.4 0.1 fusion.16
  141.6 11.4 %fusion = f32[24,32,2,4608]{3,1,2,0:T(8,128)} fusion(bf16[8,2,8,4608]{3,2,1,0:T(8,128)(2,1)S(1)} %bitcast.71, f32[64,24,32]{0,2,1:T(8,128)S(1)} %get-tuple-element.21, f32[64]{0:T(128)S(1)} %log_add_fusion), kind=kOutput, calls=%fused_computation.9 | convolution fusion | flops 906067968 | bytes 29688064 | tf_op jit(solution)/shard_map/dot_general | solution.py:80
  153.0 0.1 fusion.36
  153.1 1.6 fusion.7
  154.8 10.6 %add_reduce_fusion = (f32[32,4608]{1,0:T(8,128)S(1)}, f32[32,4608]{1,0:T(8,128)S(1)}) fusion(f32[24,32,2,4608]{3,1,2,0:T(8,128)} %fusion, f32[24,4608]{1,0:T(8,128)} %copy-done.2, f32[24,4608]{1,0:T(8,128)S(1)} %get-tuple-element.16), kind=kLoop, calls=%fused_computation.4 | loop fusion | flops 28016640 | bytes 30375936 | tf_op jit(solution)/shard_map/reduce_sum | solution.py:89
  165.4 1.1 pad_maximum_fusion.1
  166.5 0.6 add_subtract_fusion
  167.1 15.9 %reduce-scatter.5.cloned.1.call-done = f32[32,1152]{1,0:T(8,128)} async-done(((f32[32,4608]{1,0:T(8,128)}), f32[32,1152]{1,0:T(8,128)}) %reduce-scatter.5.cloned.1.call-update) | async-done | bytes 147472 | tf_op jit(solution)/shard_map/reduce_scatter | solution.py:95
  183.1 0.9 broadcast_add_fusion
  184.0 27.4 %reduce-scatter.3.cloned.1.call-done = f32[32,2,1152]{2,0,1:T(8,128)} async-done(((f32[32,2,4608]{2,0,1:T(8,128)}), f32[32,2,1152]{2,0,1:T(8,128)}) %reduce-scatter.3.cloned.1.call-update) | async-done | bytes 294928 | tf_op jit(solution)/shard_map/reduce_scatter | solution.py:94
  211.4 1.0 broadcast_divide_fusion
  212.4 0.9 copy.20
  (17 shorter events, 0.2 us)
Async XLA Ops:
  7.2 109.9 %all-gather.2.cloned.1.call-start = ((), (), s32[]{:S(2)}) async-start(), calls=%async_computation.2 | async-start | bytes 1474560 | tf_op jit(solution)/shard_map/all_gather | solution.py:59
  11.0 172.0 %reduce-scatter.5.cloned.1.call-start = ((), (), s32[]{:S(2)}) async-start(), calls=%async_computation.4 | async-start | bytes 737280 | tf_op jit(solution)/shard_map/reduce_scatter | solution.py:95
  16.0 30.8 %copy-start.2 = (f32[24,4608]{1,0:T(8,128)}, f32[24,4608]{1,0:T(8,128)S(1)}, u32[]{:S(2)}) copy-start(f32[24,4608]{1,0:T(8,128)S(1)} %get-tuple-element.17) | copy-start | bytes 1327108
  81.6 22.7 %copy-start.4 = (s32[16]{0:T(128)S(1)}, s32[16]{0:T(128)}, u32[]{:S(2)}) copy-start(s32[16]{0:T(128)} %param.10) | copy-start | bytes 196
  81.6 34.1 %copy-start = (f32[64,4608]{1,0:T(8,128)S(1)}, f32[64,4608]{1,0:T(8,128)}, u32[]{:S(2)}) copy-start(f32[64,4608]{1,0:T(8,128)} %param.8) | copy-start | bytes 3538948
  81.6 34.1 %copy-start.3 = (f32[4608]{0:T(1024)S(1)}, f32[4608]{0:T(1024)}, u32[]{:S(2)}) copy-start(f32[4608]{0:T(1024)} %param.9) | copy-start | bytes 55300
  117.0 24.5 %copy-start.1 = (bf16[64,9216]{1,0:T(8,128)(2,1)S(1)}, bf16[64,9216]{1,0:T(8,128)(2,1)}, u32[]{:S(2)}) copy-start(bf16[64,9216]{1,0:T(8,128)(2,1)} %all-gather.2.cloned.1.call-done) | copy-start | bytes 3538948
  154.7 56.7 %reduce-scatter.3.cloned.1.call-start = ((), (), s32[]{:S(2)}) async-start(), calls=%async_computation.3 | async-start | bytes 1474560 | tf_op jit(solution)/shard_map/reduce_scatter | solution.py:94
Sparse Core Ops, SparseCore 0:
  11.2 31.9 all-gather.1
  154.8 28.1 reduce-scatter.4
  185.6 25.7 reduce-scatter.2
where the time goes:
time: 221 us; the launch traced here: 220 us
  other arithmetic  84 us (38%)
  waiting for transfers between devices  43.4 us (20%)
  blocking collectives  28 us (13%)
  local copies, waits for them, and re-layouts  26.8 us (12%)
  matrix products  23.7 us (11%)
  between operations  13.9 us (6%)
    another operation x1, other arithmetic, local(): jnp.stack([temp_re, temp_im], axis=2).astype(jnp.bfloat16)  34.8 us
    another operation x1, other arithmetic  30.8 us
    reduce_scatter x1, waiting for transfers between devices, local(): lax.psum_scatter(numer, 'img', scatter_dimension=2, tiled=True)  27.4 us
    convert_element_type x1, local copies, waits for them, and re-layouts, local(): templates = jnp.stack([temp_re, temp_im], axis=2).astype(jnp.bfloat16).re...  22.7 us
    reduce_scatter x1, waiting for transfers between devices, local(): lax.psum_scatter(denom, 'img', scatter_dimension=1, tiled=True)  15.9 us
    dot_general x1, matrix products, local(): lax.dot_general(rho_low, gathered, (((0,), (0,)), ((), ())), preferred_el...  11.4 us
    all_gather x1, blocking collectives, local(): lax.all_gather(marks_low, 'cls', axis=0, tiled=True)  11.3 us
    reduce_sum x1, other arithmetic, local(): jnp.sum(sums[:, :, 0, :] * cos_b + sums[:, :, 1, :] * sin_b, axis=0)  10.6 us
  transfers between devices with their start and end apart: 3, of which 2 were waited for; matrix products, arithmetic and copies ran while one was open for 49% of the time, Pallas kernels for 0%

commit v1 on v0

v1 whole, which is shorter than its diff:
```python
import functools

import jax
import jax.numpy as jnp
from jax import lax
from jax.experimental import pallas as pl
from jax.experimental.pallas import tpu as pltpu
from jax.sharding import PartitionSpec as P

BOX = 128
LANES = 128
MESH = pl.DeviceIdType.MESH
HIGHEST = lax.Precision.HIGHEST
NT = (((1,), (1,)), ((), ()))

prior_precision = 0.02


def phase_tables(shifts, freq):
    step = 2.0 * jnp.pi / BOX
    along_y = jnp.arange(freq // BOX).astype(jnp.float32)
    along_x = (jnp.arange(BOX) - BOX // 2).astype(jnp.float32)
    angle_x = step * (shifts[:, 0:1].astype(jnp.float32) * along_x[None, :])
    angle_y = step * (shifts[:, 1:2].astype(jnp.float32) * along_y[None, :])
    cos_x, sin_x = jnp.cos(angle_x)[:, None, :], jnp.sin(angle_x)[:, None, :]
    cos_y, sin_y = jnp.cos(angle_y)[:, :, None], jnp.sin(angle_y)[:, :, None]
    shape = (shifts.shape[0], freq)
    return (
        (cos_x * cos_y - sin_x * sin_y).reshape(shape),
        (sin_x * cos_y + cos_x * sin_y).reshape(shape),
    )


def kernel(
    n_cls, n_img, chunk,
    ids_s, ids_v, part_ref, cls_ref, ctf_ref, nw_ref, cos_ref, sin_ref,
    resp_ref, avg_ref,
    wbuf, sel, temps, scores, rho_low, stat, mass_buf, send_buf, recv_buf, own,
    gs_sem, gr_sem, ss_sem, sr_sem, ms_sem, mr_sem, ns_sem, nr_sem,
):
    rows = part_ref.shape[0]
    freq = ctf_ref.shape[1]
    groups = ctf_ref.shape[0]
    classes = cls_ref.shape[0]
    poses = cos_ref.shape[0]
    total = rows * n_cls
    part_freq = freq // n_img
    my_cls = lax.axis_index("cls")
    my_img = lax.axis_index("img")

    barrier = pltpu.get_barrier_semaphore()
    for d in range(1, n_cls):
        pl.semaphore_signal(
            barrier, inc=1, device_id={"cls": lax.rem(my_cls + d, n_cls)}, device_id_type=MESH
        )
    for d in range(1, n_img):
        pl.semaphore_signal(
            barrier, inc=1, device_id={"img": lax.rem(my_img + d, n_img)}, device_id_type=MESH
        )

    for i in range(rows):
        sel[pl.ds(i, 1), :] = ctf_ref[pl.ds(ids_s[i], 1), :] * nw_ref[...]
    for part in range(2):
        cols = slice(part * freq, (part + 1) * freq)
        wbuf[my_cls, :, cols] = (
            part_ref[:, cols].astype(jnp.float32) * sel[...]
        ).astype(jnp.bfloat16)
    pad_groups = wbuf.shape[2] - 2 * freq
    wbuf[my_cls, :, 2 * freq :] = (
        ids_v[...] == lax.broadcasted_iota(jnp.int32, (rows, pad_groups), 1)
    ).astype(jnp.float32).astype(jnp.bfloat16)

    pl.semaphore_wait(barrier, n_cls + n_img - 2)

    def gather_copy(d, slot):
        return pltpu.make_async_remote_copy(
            src_ref=wbuf.at[slot],
            dst_ref=wbuf.at[slot],
            send_sem=gs_sem.at[d],
            recv_sem=gr_sem.at[d],
            device_id={"cls": lax.rem(my_cls + d, n_cls)},
            device_id_type=MESH,
        )

    for d in range(1, n_cls):
        gather_copy(d, my_cls).start()

    def build(c, power):
        at = pl.multiple_of(c * chunk, LANES)
        at_im = pl.multiple_of(freq + c * chunk, LANES)
        re = cls_ref[:, pl.ds(at, chunk)].astype(jnp.float32)
        im = cls_ref[:, pl.ds(at_im, chunk)].astype(jnp.float32)
        for r in range(poses):
            cos_r = cos_ref[r : r + 1, pl.ds(at, chunk)]
            sin_r = sin_ref[r : r + 1, pl.ds(at, chunk)]
            out = slice(r * classes, (r + 1) * classes)
            temps[out, pl.ds(at, chunk)] = (re * cos_r - im * sin_r).astype(jnp.bfloat16)
            temps[out, pl.ds(at_im, chunk)] = (re * sin_r + im * cos_r).astype(jnp.bfloat16)
        ctf = ctf_ref[:, pl.ds(at, chunk)]
        weight = ctf * ctf * nw_ref[:, pl.ds(at, chunk)]
        return power + lax.dot_general(
            re * re + im * im, weight, NT, precision=HIGHEST,
            preferred_element_type=jnp.float32,
        )

    power = lax.fori_loop(
        0, freq // chunk, build, jnp.zeros((classes, groups), jnp.float32)
    )

    for d in range(1, n_cls):
        gather_copy(d, lax.rem(my_cls + n_cls - d, n_cls)).wait_recv()

    marks = wbuf[:, :, 2 * freq :].reshape(total, pad_groups)[:, :groups].astype(jnp.float32)
    penalty = lax.dot_general(
        power, marks, NT, precision=HIGHEST, preferred_element_type=jnp.float32
    )
    scores[...] = jnp.zeros_like(scores)

    def cross(c, carry):
        at = pl.multiple_of(c * 2 * chunk, LANES)
        scores[...] += lax.dot_general(
            temps[:, pl.ds(at, 2 * chunk)],
            wbuf[:, :, pl.ds(at, 2 * chunk)].reshape(total, 2 * chunk),
            NT,
            preferred_element_type=jnp.float32,
        )
        return carry

    lax.fori_loop(0, freq // chunk, cross, 0)

    value = scores[...].reshape(poses, classes, total) - 0.5 * penalty[None]
    pose_peak = jnp.max(value, axis=0)
    pose_sum = jnp.sum(jnp.exp(value - pose_peak[None]), axis=0)
    peak = jnp.max(pose_peak, axis=0, keepdims=True)
    stat[0, 0:1, :total] = peak
    stat[0, 1:2, :total] = jnp.sum(
        pose_sum * jnp.exp(pose_peak - peak), axis=0, keepdims=True
    )

    def stat_copy(d):
        return pltpu.make_async_remote_copy(
            src_ref=stat.at[0],
            dst_ref=stat.at[d],
            send_sem=ss_sem.at[d],
            recv_sem=sr_sem.at[d],
            device_id={"cls": lax.rem(my_cls + d, n_cls)},
            device_id_type=MESH,
        )

    for d in range(1, n_cls):
        stat_copy(d).start()
    for d in range(1, n_cls):
        stat_copy(d).wait_recv()
    whole_peak = peak
    for d in range(1, n_cls):
        whole_peak = jnp.maximum(whole_peak, stat[d, 0:1, :total])
    norm = jnp.zeros_like(peak)
    for d in range(n_cls):
        norm += stat[d, 1:2, :total] * jnp.exp(stat[d, 0:1, :total] - whole_peak)
    log_norm = whole_peak + jnp.log(norm)
    resp_ref[...] = pose_peak + jnp.log(pose_sum) - log_norm
    rho = jnp.exp(value - log_norm[None])
    rho_low[...] = rho.reshape(poses * classes, total).astype(jnp.bfloat16)
    mass_buf[0] = jnp.dot(
        jnp.sum(rho, axis=0),
        wbuf[:, :, 2 * freq :].reshape(total, pad_groups).astype(jnp.float32),
        precision=HIGHEST,
        preferred_element_type=jnp.float32,
    )

    def to_img(src, dst, d, send, recv):
        return pltpu.make_async_remote_copy(
            src_ref=src.at[d] if src is send_buf else src.at[0],
            dst_ref=dst.at[d],
            send_sem=send.at[d],
            recv_sem=recv.at[d],
            device_id={"img": lax.rem(my_img + d, n_img)},
            device_id_type=MESH,
        )

    for d in range(1, n_img):
        to_img(mass_buf, mass_buf, d, ms_sem, mr_sem).start()

    def numer(target, store):
        def step(c, carry):
            at = pl.multiple_of(target * part_freq + c * chunk, LANES)
            at_im = pl.multiple_of(freq + target * part_freq + c * chunk, LANES)
            low = rho_low[...]
            sum_re = jnp.dot(
                low, wbuf[:, :, pl.ds(at, chunk)].reshape(total, chunk),
                preferred_element_type=jnp.float32,
            )
            sum_im = jnp.dot(
                low, wbuf[:, :, pl.ds(at_im, chunk)].reshape(total, chunk),
                preferred_element_type=jnp.float32,
            )
            acc_re = jnp.zeros((classes, chunk), jnp.float32)
            acc_im = jnp.zeros((classes, chunk), jnp.float32)
            for r in range(poses):
                cos_r = cos_ref[r : r + 1, pl.ds(at, chunk)]
                sin_r = sin_ref[r : r + 1, pl.ds(at, chunk)]
                s_re = sum_re[r * classes : (r + 1) * classes]
                s_im = sum_im[r * classes : (r + 1) * classes]
                acc_re += s_re * cos_r + s_im * sin_r
                acc_im += s_im * cos_r - s_re * sin_r
            store(pl.multiple_of(c * chunk, LANES), acc_re, acc_im)
            return carry

        lax.fori_loop(0, part_freq // chunk, step, 0)

    for d in range(1, n_img):
        def store_peer(at, re, im, d=d):
            send_buf[d, :classes, pl.ds(at, chunk)] = re.astype(send_buf.dtype)
            send_buf[d, classes:, pl.ds(at, chunk)] = im.astype(send_buf.dtype)

        numer(lax.rem(my_img + d, n_img), store_peer)
        to_img(send_buf, recv_buf, d, ns_sem, nr_sem).start()

    def store_own(at, re, im):
        own[:classes, pl.ds(at, chunk)] = re
        own[classes:, pl.ds(at, chunk)] = im

    numer(my_img, store_own)

    for d in range(1, n_img):
        to_img(mass_buf, mass_buf, d, ms_sem, mr_sem).wait_recv()
    mass = mass_buf[0]
    for d in range(1, n_img):
        mass += mass_buf[d]
    mine = pl.ds(pl.multiple_of(my_img * part_freq, LANES), part_freq)
    ctf = ctf_ref[:, mine]
    denom = jnp.dot(
        mass[:, :groups], ctf * ctf * nw_ref[:, mine], precision=HIGHEST,
        preferred_element_type=jnp.float32,
    ) + prior_precision

    for d in range(1, n_img):
        to_img(send_buf, recv_buf, d, ns_sem, nr_sem).wait_recv()
    for part in range(2):
        at = slice(part * classes, (part + 1) * classes)
        value_sum = own[at]
        for d in range(1, n_img):
            value_sum += recv_buf[d, at].astype(jnp.float32)
        avg_ref[part] = value_sum / denom

    for d in range(1, n_cls):
        gather_copy(d, my_cls).wait_send()
        stat_copy(d).wait_send()
    for d in range(1, n_img):
        to_img(mass_buf, mass_buf, d, ms_sem, mr_sem).wait_send()
        to_img(send_buf, recv_buf, d, ns_sem, nr_sem).wait_send()


def local(n_cls, n_img, particles, classes, ctf, noise_weight, group_ids, shifts):
    rows, _, freq = particles.shape
    cls_rows = classes.shape[0]
    poses = shifts.shape[0]
    groups = ctf.shape[0]
    total = rows * n_cls
    part_freq = freq // n_img
    chunk = 384 if part_freq % 384 == 0 else LANES
    pad_groups = -(-groups // LANES) * LANES
    pad_total = -(-total // LANES) * LANES
    cos_t, sin_t = phase_tables(shifts, freq)
    vmem = pl.BlockSpec(memory_space=pltpu.VMEM)
    dma = pltpu.SemaphoreType.DMA
    resp, avg = pl.pallas_call(
        functools.partial(kernel, n_cls, n_img, chunk),
        out_shape=(
            jax.ShapeDtypeStruct((cls_rows, total), jnp.float32),
            jax.ShapeDtypeStruct((2, cls_rows, part_freq), jnp.float32),
        ),
        in_specs=[pl.BlockSpec(memory_space=pltpu.SMEM)] + [vmem] * 7,
        out_specs=(vmem, vmem),
        scratch_shapes=[
            pltpu.VMEM((n_cls, rows, 2 * freq + pad_groups), jnp.bfloat16),
            pltpu.VMEM((rows, freq), jnp.float32),
            pltpu.VMEM((poses * cls_rows, 2 * freq), jnp.bfloat16),
            pltpu.VMEM((poses * cls_rows, total), jnp.float32),
            pltpu.VMEM((poses * cls_rows, total), jnp.bfloat16),
            pltpu.VMEM((n_cls, 8, pad_total), jnp.float32),
            pltpu.VMEM((n_img, cls_rows, pad_groups), jnp.float32),
            pltpu.VMEM((n_img, 2 * cls_rows, part_freq), jnp.bfloat16),
            pltpu.VMEM((n_img, 2 * cls_rows, part_freq), jnp.bfloat16),
            pltpu.VMEM((2 * cls_rows, part_freq), jnp.float32),
            dma((n_cls,)), dma((n_cls,)), dma((n_cls,)), dma((n_cls,)),
            dma((n_img,)), dma((n_img,)), dma((n_img,)), dma((n_img,)),
        ],
        compiler_params=pltpu.CompilerParams(
            collective_id=0, has_side_effects=True, vmem_limit_bytes=56 << 20
        ),
    )(
        group_ids,
        group_ids[:, None],
        particles.reshape(rows, 2 * freq),
        classes.reshape(cls_rows, 2 * freq),
        ctf,
        noise_weight[None, :],
        cos_t,
        sin_t,
    )
    return resp.T, avg.transpose(1, 0, 2)


def solution(mesh):
    placed = (
        P(("groups", "img", "cls"), None, None),
        P(("groups", "cls"), None, None),
        P("groups", None),
        P("groups"),
        P(("groups", "img", "cls")),
        P("groups", None),
    )
    return jax.shard_map(
        functools.partial(local, mesh.shape["cls"], mesh.shape["img"]),
        mesh=mesh,
        in_specs=placed,
        out_specs=(P(("groups", "img"), "cls"), P(("groups", "cls"), None, "img")),
        check_vma=False,
    )
```

time: 221 us -> 63.4 us (0.29)
  other arithmetic: 84 us -> 1.34 us
  Pallas kernels: 0 us -> 53.9 us
  waiting for transfers between devices: 43.4 us -> 0 us
  blocking collectives: 28 us -> 0 us
  matrix products: 23.7 us -> 0 us
  local copies, waits for them, and re-layouts: 26.8 us -> 7.24 us
  between operations: 13.9 us -> 0.68 us
    another operation x3 -> x0, other arithmetic: 66.7 us -> none  [the longest x1 34.8 us: local(): jnp.stack([temp_re, temp_im], axis=2).astype(jnp.bfloat16)]
    pallas_call x0 -> x1, Pallas kernels: none -> 53.9 us  [local(): pl.pallas_call(functools.partial(kernel, n_cls, n_img, chunk), out_shape=...]
    reduce_scatter x2 -> x0, waiting for transfers between devices: 43.3 us -> none  [the longest x1 27.4 us: local(): lax.psum_scatter(numer, 'img', scatter_dimension=2, tiled=True)]
    dot_general x7 -> x0, matrix products: 23.7 us -> none  [the longest x1 11.4 us: local(): lax.dot_general(rho_low, gathered, (((0,), (0,)), ((), ())), preferred_el...]
    convert_element_type x1 -> x0, local copies, waits for them, and re-layouts: 22.7 us -> none  [local(): templates = jnp.stack([temp_re, temp_im], axis=2).astype(jnp.bfloat16).re...]
    all_gather x1 -> x0, blocking collectives: 11.3 us -> none  [local(): lax.all_gather(marks_low, 'cls', axis=0, tiled=True)]
    reduce_sum x3 -> x0, other arithmetic: 10.9 us -> none  [the longest x1 10.6 us: local(): jnp.sum(sums[:, :, 0, :] * cos_b + sums[:, :, 1, :] * sin_b, axis=0)]
    pmax x1 -> x0, blocking collectives: 9.9 us -> none  [local(): peak = lax.pmax(local_peak, 'cls')]
  transfers between devices with their start and end apart: 3 -> 0, of which waited for: 2 -> 0; matrix products, arithmetic and copies ran while one was open for 49% -> 0% of each run, Pallas kernels for 0% -> 0%
where the time goes in v1:
time: 63.4 us; the launch traced here: 63.1 us
  Pallas kernels  53.9 us (85%)
  local copies, waits for them, and re-layouts  7.24 us (11%)
  other arithmetic  1.34 us (2%)
  between operations  0.68 us (1%)
    pallas_call x1, Pallas kernels, local(): pl.pallas_call(functools.partial(kernel, n_cls, n_img, chunk), out_shape=...  53.9 us
    unnamed x12, local copies, waits for them, and re-layouts  4.87 us

profile of v1, /device:TPU:1, one launch (start us, length us, event | category | flops | bytes accessed | tf_op | source)
XLA Modules:
  0.0 63.1 jit_solution(15410146693967313696)
XLA Ops:
  0.6 0.8 %convert_bitcast_fusion.1 = (f32[24]{0:T(128)S(1)}, f32[24]{0:T(128)S(1)}) fusion(s32[24,2]{0,1:T(2,128)} %param.11), kind=kLoop, calls=%fused_computation.13 | loop fusion | flops 48 | bytes 384 | tf_op jit(solution)/shard_map/mul | solution.py:23
  1.4 0.1 fusion.3
  1.5 0.1 fusion.1
  1.7 0.3 multiply_add_fusion
  2.0 0.0 copy-start
  2.0 0.0 copy-start.1
  2.0 1.1 %copy_bitcast_fusion = (f32[24,4608]{1,0:T(8,128)}, f32[24,4608]{1,0:T(8,128)}) fusion(f32[3,8,36,128]{3,2,1,0:T(8,128)S(1)} %bitcast.18, f32[3,8,36,128]{3,2,1,0:T(8,128)S(1)} %bitcast.19), kind=kLoop, calls=%fused_computation.2 | loop fusion | bytes 1769472 | tf_op jit(solution)/shard_map/add | solution.py:30
  3.1 0.0 copy-start.2
  3.1 0.0 copy-start.3
  3.1 0.0 copy-done
  3.1 0.9 %copy.13 = bf16[4,8,2,4608]{3,1,2,0:T(8,128)(2,1)} copy(bf16[4,8,2,4608]{3,2,1,0:T(2,128)(2,1)S(1)} %bitcast.21) | data formatting | bytes 1179648
  4.0 0.0 copy-done.1
  4.0 0.7 %copy.12 = bf16[2,8,2,4608]{3,1,2,0:T(8,128)(2,1)} copy(bf16[2,8,2,4608]{3,2,1,0:T(2,128)(2,1)S(1)} %bitcast.22) | data formatting | bytes 589824
  4.7 0.0 copy-done.2
  4.7 0.6 broadcast_in_dim.5.nw_ref
  5.3 0.0 copy-done.3
  5.3 0.7 %copy.10.ids_v = s32[16,1]{1,0:T(8,128)} copy(s32[16,1]{0,1:T(1,128)S(1)} %bitcast.25) | data formatting | bytes 128 | tf_op jit(solution)/shard_map/broadcast_in_dim | solution.py:294
  6.0 53.9 %shard_map.77 = (f32[32,64]{1,0:T(8,128)}, f32[2,32,1152]{2,1,0:T(8,128)}) custom-call(s32[16]{0:T(128)} %ids_s.1, s32[16,1]{1,0:T(8,128)} %copy.10.ids_v, bf16[16,9216]{1,0:T(8,128)(2,1)} %bitcast.20, bf16[32,9216]{1,0:T(8,128)(2,1)} %bitcast.17, f32[64,4608]{1,0:T(8,128)} %ctf_ref.1, f32[1,4608]{1,0:T(1,128)} %broadcast_in_dim.5.nw_ref, ...), custom_call_target="tpu_custom_call" | custom-call | tf_op jit(solution)/shard_map/pallas_call | solution.py:267
  59.9 1.9 %copy.11 = f32[32,2,1152]{2,1,0:T(2,128)} copy(f32[32,2,1152]{2,0,1:T(8,128)} %bitcast.23) | data formatting | bytes 589824
  61.8 1.3 %copy.19 = f32[64,32]{0,1:T(8,128)} copy(f32[64,32]{0,1:T(8,128)} %bitcast.24) | data formatting | bytes 16384
  (2 shorter events, 0.0 us)
Async XLA Ops:
  2.0 1.1 %copy-start = (bf16[32,2,4608]{2,1,0:T(2,128)(2,1)S(1)}, bf16[32,2,4608]{2,1,0:T(2,128)(2,1)}, u32[]{:S(2)}) copy-start(bf16[32,2,4608]{2,1,0:T(2,128)(2,1)} %param.7) | copy-start | bytes 1769476
  2.0 2.0 %copy-start.1 = (bf16[16,2,4608]{2,1,0:T(2,128)(2,1)S(1)}, bf16[16,2,4608]{2,1,0:T(2,128)(2,1)}, u32[]{:S(2)}) copy-start(bf16[16,2,4608]{2,1,0:T(2,128)(2,1)} %param.6) | copy-start | bytes 884740
  3.1 1.6 %copy-start.2 = (f32[4608]{0:T(1024)S(1)}, f32[4608]{0:T(1024)}, u32[]{:S(2)}) copy-start(f32[4608]{0:T(1024)} %param.9) | copy-start | bytes 55300
  3.1 2.2 %copy-start.3 = (s32[16]{0:T(128)S(1)}, s32[16]{0:T(128)}, u32[]{:S(2)}) copy-start(s32[16]{0:T(128)} %ids_s.1) | copy-start | bytes 196

commit v2 on v1

--- a/solution.py
+++ b/solution.py
@@ -16,27 +16,31 @@
 prior_precision = 0.02
 
 
-def phase_tables(shifts, freq):
+def fill_phase_tables(shifts, cos_ref, sin_ref):
+    poses, freq = cos_ref.shape
     step = 2.0 * jnp.pi / BOX
-    along_y = jnp.arange(freq // BOX).astype(jnp.float32)
-    along_x = (jnp.arange(BOX) - BOX // 2).astype(jnp.float32)
-    angle_x = step * (shifts[:, 0:1].astype(jnp.float32) * along_x[None, :])
-    angle_y = step * (shifts[:, 1:2].astype(jnp.float32) * along_y[None, :])
-    cos_x, sin_x = jnp.cos(angle_x)[:, None, :], jnp.sin(angle_x)[:, None, :]
-    cos_y, sin_y = jnp.cos(angle_y)[:, :, None], jnp.sin(angle_y)[:, :, None]
-    shape = (shifts.shape[0], freq)
-    return (
-        (cos_x * cos_y - sin_x * sin_y).reshape(shape),
-        (sin_x * cos_y + cos_x * sin_y).reshape(shape),
-    )
+    lane = lax.broadcasted_iota(jnp.int32, (poses, BOX), 1)
+    move_x = shifts[:, 0:1].astype(jnp.float32)
+    move_y = shifts[:, 1:2].astype(jnp.float32)
+    angle_x = step * (move_x * (lane - BOX // 2).astype(jnp.float32))
+    cos_x, sin_x = jnp.cos(angle_x), jnp.sin(angle_x)
+    for row in range(freq // BOX):
+        if row % BOX == 0:
+            angle_y = step * (move_y * (lane + row).astype(jnp.float32))
+            cos_rows, sin_rows = jnp.cos(angle_y), jnp.sin(angle_y)
+        cos_y = cos_rows[:, row % BOX : row % BOX + 1]
+        sin_y = sin_rows[:, row % BOX : row % BOX + 1]
+        cols = slice(row * BOX, (row + 1) * BOX)
+        cos_ref[:, cols] = cos_x * cos_y - sin_x * sin_y
+        sin_ref[:, cols] = sin_x * cos_y + cos_x * sin_y
 
 
 def kernel(
-    n_cls, n_img, chunk,
-    ids_s, ids_v, part_ref, cls_ref, ctf_ref, nw_ref, cos_ref, sin_ref,
+    n_cls, n_img, chunk, pieces,
+    ids_s, part_ref, cls_ref, ctf_ref, nw_ref, shift_ref,
     resp_ref, avg_ref,
-    wbuf, sel, temps, scores, rho_low, stat, mass_buf, send_buf, recv_buf, own,
-    gs_sem, gr_sem, ss_sem, sr_sem, ms_sem, mr_sem, ns_sem, nr_sem,
+    wbuf, sel, onehot, cos_ref, sin_ref, temps, scores, rho_low, stat, mass_buf, send_buf, recv_buf, own,
+    right_sem, left_sem, gr_sem, ss_sem, sr_sem, ms_sem, mr_sem, ns_sem, nr_sem,
 ):
     rows = part_ref.shape[0]
     freq = ctf_ref.shape[1]
@@ -60,30 +64,62 @@
 
     for i in range(rows):
         sel[pl.ds(i, 1), :] = ctf_ref[pl.ds(ids_s[i], 1), :] * nw_ref[...]
+        onehot[pl.ds(i, 1), :] = (
+            lax.broadcasted_iota(jnp.int32, (1, onehot.shape[1]), 1) == ids_s[i]
+        ).astype(jnp.float32)
     for part in range(2):
         cols = slice(part * freq, (part + 1) * freq)
         wbuf[my_cls, :, cols] = (
             part_ref[:, cols].astype(jnp.float32) * sel[...]
         ).astype(jnp.bfloat16)
     pad_groups = wbuf.shape[2] - 2 * freq
-    wbuf[my_cls, :, 2 * freq :] = (
-        ids_v[...] == lax.broadcasted_iota(jnp.int32, (rows, pad_groups), 1)
-    ).astype(jnp.float32).astype(jnp.bfloat16)
+    wbuf[my_cls, :, 2 * freq :] = onehot[...].astype(jnp.bfloat16)
 
     pl.semaphore_wait(barrier, n_cls + n_img - 2)
 
-    def gather_copy(d, slot):
+    width = 2 * freq // pieces
+
+    def hop(slot, p, to_right):
+        last = pad_groups if p == pieces - 1 else 0
+        cols = pl.ds(p * width, width + last)
         return pltpu.make_async_remote_copy(
-            src_ref=wbuf.at[slot],
-            dst_ref=wbuf.at[slot],
-            send_sem=gs_sem.at[d],
-            recv_sem=gr_sem.at[d],
-            device_id={"cls": lax.rem(my_cls + d, n_cls)},
+            src_ref=wbuf.at[slot, :, cols],
+            dst_ref=wbuf.at[slot, :, cols],
+            send_sem=(right_sem if to_right else left_sem).at[slot, p],
+            recv_sem=gr_sem.at[slot, p],
+            device_id={"cls": my_cls + 1 if to_right else my_cls - 1},
             device_id_type=MESH,
         )
 
-    for d in range(1, n_cls):
-        gather_copy(d, my_cls).start()
+    has_right = my_cls < n_cls - 1
+    has_left = my_cls > 0
+
+    def start_right(slot, p):
+        @pl.when(has_right)
+        def _():
+            hop(slot, p, True).start()
+
+    def start_left(slot, p):
+        @pl.when(has_left)
+        def _():
+            hop(slot, p, False).start()
+
+    def relay(h, p):
+        @pl.when(my_cls - h >= 0)
+        def _():
+            hop(my_cls - h, p, False).wait_recv()
+            start_right(my_cls - h, p)
+
+        @pl.when(my_cls + h < n_cls)
+        def _():
+            hop(my_cls + h, p, True).wait_recv()
+            start_left(my_cls + h, p)
+
+    for p in range(pieces):
+        start_right(my_cls, p)
+        start_left(my_cls, p)
+
+    fill_phase_tables(shift_ref[...], cos_ref, sin_ref)
 
     def build(c, power):
         at = pl.multiple_of(c * chunk, LANES)
@@ -107,14 +143,16 @@
         0, freq // chunk, build, jnp.zeros((classes, groups), jnp.float32)
     )
 
-    for d in range(1, n_cls):
-        gather_copy(d, lax.rem(my_cls + n_cls - d, n_cls)).wait_recv()
-
-    marks = wbuf[:, :, 2 * freq :].reshape(total, pad_groups)[:, :groups].astype(jnp.float32)
-    penalty = lax.dot_general(
-        power, marks, NT, precision=HIGHEST, preferred_element_type=jnp.float32
-    )
     scores[...] = jnp.zeros_like(scores)
+
+    def relay_all(h, carry):
+        for p in range(pieces):
+            relay(h, p)
+        return carry
+
+    lax.fori_loop(1, n_cls - 1, relay_all, 0)
+
+    steps = width // (2 * chunk)
 
     def cross(c, carry):
         at = pl.multiple_of(c * 2 * chunk, LANES)
@@ -126,8 +164,14 @@
         )
         return carry
 
-    lax.fori_loop(0, freq // chunk, cross, 0)
-
+    for p in range(pieces):
+        relay(n_cls - 1, p)
+        lax.fori_loop(p * steps, (p + 1) * steps, cross, 0)
+
+    marks = wbuf[:, :, 2 * freq :].reshape(total, pad_groups)[:, :groups].astype(jnp.float32)
+    penalty = lax.dot_general(
+        power, marks, NT, precision=HIGHEST, preferred_element_type=jnp.float32
+    )
     value = scores[...].reshape(poses, classes, total) - 0.5 * penalty[None]
     pose_peak = jnp.max(value, axis=0)
     pose_sum = jnp.sum(jnp.exp(value - pose_peak[None]), axis=0)
@@ -244,8 +288,20 @@
         avg_ref[part] = value_sum / denom
 
     for d in range(1, n_cls):
-        gather_copy(d, my_cls).wait_send()
         stat_copy(d).wait_send()
+
+    def drain(h, carry):
+        for p in range(pieces):
+            @pl.when(has_right & (my_cls - h >= 0))
+            def _(p=p):
+                hop(my_cls - h, p, True).wait_send()
+
+            @pl.when(has_left & (my_cls + h < n_cls))
+            def _(p=p):
+                hop(my_cls + h, p, False).wait_send()
+        return carry
+
+    lax.fori_loop(0, n_cls - 1, drain, 0)
     for d in range(1, n_img):
         to_img(mass_buf, mass_buf, d, ms_sem, mr_sem).wait_send()
         to_img(send_buf, recv_buf, d, ns_sem, nr_sem).wait_send()
@@ -261,20 +317,23 @@
     chunk = 384 if part_freq % 384 == 0 else LANES
     pad_groups = -(-groups // LANES) * LANES
     pad_total = -(-total // LANES) * LANES
-    cos_t, sin_t = phase_tables(shifts, freq)
+    pieces = next(p for p in (4, 3, 2, 1) if 2 * freq % (p * 2 * chunk) == 0)
     vmem = pl.BlockSpec(memory_space=pltpu.VMEM)
     dma = pltpu.SemaphoreType.DMA
     resp, avg = pl.pallas_call(
-        functools.partial(kernel, n_cls, n_img, chunk),
+        functools.partial(kernel, n_cls, n_img, chunk, pieces),
         out_shape=(
             jax.ShapeDtypeStruct((cls_rows, total), jnp.float32),
             jax.ShapeDtypeStruct((2, cls_rows, part_freq), jnp.float32),
         ),
-        in_specs=[pl.BlockSpec(memory_space=pltpu.SMEM)] + [vmem] * 7,
+        in_specs=[pl.BlockSpec(memory_space=pltpu.SMEM)] + [vmem] * 5,
         out_specs=(vmem, vmem),
         scratch_shapes=[
             pltpu.VMEM((n_cls, rows, 2 * freq + pad_groups), jnp.bfloat16),
             pltpu.VMEM((rows, freq), jnp.float32),
+            pltpu.VMEM((rows, pad_groups), jnp.float32),
+            pltpu.VMEM((poses, freq), jnp.float32),
+            pltpu.VMEM((poses, freq), jnp.float32),
             pltpu.VMEM((poses * cls_rows, 2 * freq), jnp.bfloat16),
             pltpu.VMEM((poses * cls_rows, total), jnp.float32),
             pltpu.VMEM((poses * cls_rows, total), jnp.bfloat16),
@@ -283,7 +342,8 @@
             pltpu.VMEM((n_img, 2 * cls_rows, part_freq), jnp.bfloat16),
             pltpu.VMEM((n_img, 2 * cls_rows, part_freq), jnp.bfloat16),
             pltpu.VMEM((2 * cls_rows, part_freq), jnp.float32),
-            dma((n_cls,)), dma((n_cls,)), dma((n_cls,)), dma((n_cls,)),
+            dma((n_cls, pieces)), dma((n_cls, pieces)), dma((n_cls, pieces)),
+            dma((n_cls,)), dma((n_cls,)),
             dma((n_img,)), dma((n_img,)), dma((n_img,)), dma((n_img,)),
         ],
         compiler_params=pltpu.CompilerParams(
@@ -291,13 +351,11 @@
         ),
     )(
         group_ids,
-        group_ids[:, None],
         particles.reshape(rows, 2 * freq),
         classes.reshape(cls_rows, 2 * freq),
         ctf,
         noise_weight[None, :],
-        cos_t,
-        sin_t,
+        shifts,
     )
     return resp.T, avg.transpose(1, 0, 2)
 

time: 63.4 us -> 54.7 us (0.86)
  Pallas kernels: 53.9 us -> 44.1 us
  local copies, waits for them, and re-layouts: 7.24 us -> 9.56 us
  other arithmetic: 1.34 us -> 0 us
    pallas_call x1, Pallas kernels: 53.9 us -> 44.1 us  [local(): pl.pallas_call(functools.partial(kernel, n_cls, n_img, chunk, pieces), ou...]
    unnamed x12 -> x5, local copies, waits for them, and re-layouts: 4.87 us -> 8.22 us
    add x1 -> x0, local copies, waits for them, and re-layouts: 1.08 us -> none  [phase_tables(): sin_x * cos_y + cos_x * sin_y]
    mul x1 -> x0, other arithmetic: 0.76 us -> none  [phase_tables(): angle_x = step * (shifts[:, 0:1].astype(jnp.float32) * along_x[None, :])]
    broadcast_in_dim x1, local copies, waits for them, and re-layouts: 0.61 us -> 1.34 us  [local(): noise_weight[None, :]]
    broadcast_in_dim x1 -> x0, local copies, waits for them, and re-layouts: 0.68 us -> none  [local(): group_ids[:, None]]
where the time goes in v2:
time: 54.7 us; the launch traced here: 54.4 us
  Pallas kernels  44.1 us (81%)
  local copies, waits for them, and re-layouts  9.56 us (17%)
  between operations  0.64 us (1%)
    pallas_call x1, Pallas kernels, local(): pl.pallas_call(functools.partial(kernel, n_cls, n_img, chunk, pieces), ou...  44.1 us
    unnamed x5, local copies, waits for them, and re-layouts  8.22 us
    broadcast_in_dim x1, local copies, waits for them, and re-layouts, local(): noise_weight[None, :]  1.34 us

profile of v2, /device:TPU:1, one launch (start us, length us, event | category | flops | bytes accessed | tf_op | source)
XLA Modules:
  0.0 54.4 jit_solution(15026309870859788336)
XLA Ops:
  0.6 1.4 %copy.8.shift_ref = s32[24,2]{1,0:T(8,128)} copy(s32[24,2]{0,1:T(2,128)} %param.11) | data formatting | bytes 384 | tf_op args[5]
  2.0 1.3 %broadcast_in_dim.3.nw_ref = f32[1,4608]{1,0:T(1,128)} reshape(f32[4608]{0:T(1024)} %param.9) | data formatting | bytes 36864 | tf_op jit(solution)/shard_map/broadcast_in_dim | solution.py:357
  3.3 1.7 %copy.10 = bf16[2,8,2,4608]{3,1,2,0:T(8,128)(2,1)} copy(bf16[2,8,2,4608]{3,2,1,0:T(2,128)(2,1)} %bitcast.9) | data formatting | bytes 589824
  5.0 1.9 %copy.11 = bf16[4,8,2,4608]{3,1,2,0:T(8,128)(2,1)} copy(bf16[4,8,2,4608]{3,2,1,0:T(2,128)(2,1)} %bitcast.8) | data formatting | bytes 1179648
  7.0 44.1 %shard_map.77 = (f32[32,64]{1,0:T(8,128)}, f32[2,32,1152]{2,1,0:T(8,128)}) custom-call(s32[16]{0:T(128)} %ids_s.1, bf16[16,9216]{1,0:T(8,128)(2,1)} %bitcast.7, bf16[32,9216]{1,0:T(8,128)(2,1)} %bitcast.6, f32[64,4608]{1,0:T(8,128)} %ctf_ref.1, f32[1,4608]{1,0:T(1,128)} %broadcast_in_dim.3.nw_ref, s32[24,2]{1,0:T(8,128)} %copy.8.shift_ref), custom_call_target="tpu_custom_call" | custom-call | tf_op jit(solution)/shard_map/pallas_call | solution.py:323
  51.1 1.9 %copy.9 = f32[32,2,1152]{2,1,0:T(2,128)} copy(f32[32,2,1152]{2,0,1:T(8,128)} %bitcast.10) | data formatting | bytes 589824
  53.0 1.3 %copy.13 = f32[64,32]{0,1:T(8,128)} copy(f32[64,32]{0,1:T(8,128)} %bitcast.11) | data formatting | bytes 16384

commit v3 on v2

--- a/solution.py
+++ b/solution.py
@@ -16,12 +16,17 @@
 prior_precision = 0.02
 
 
-def fill_phase_tables(shifts, cos_ref, sin_ref):
+def fill_phase_tables(shift_ref, cos_ref, sin_ref):
     poses, freq = cos_ref.shape
     step = 2.0 * jnp.pi / BOX
     lane = lax.broadcasted_iota(jnp.int32, (poses, BOX), 1)
-    move_x = shifts[:, 0:1].astype(jnp.float32)
-    move_y = shifts[:, 1:2].astype(jnp.float32)
+    pose = lax.broadcasted_iota(jnp.int32, (poses, BOX), 0)
+    move_x = jnp.zeros((poses, BOX), jnp.int32)
+    move_y = jnp.zeros((poses, BOX), jnp.int32)
+    for r in range(poses):
+        move_x = jnp.where(pose == r, shift_ref[0, r], move_x)
+        move_y = jnp.where(pose == r, shift_ref[1, r], move_y)
+    move_x, move_y = move_x.astype(jnp.float32), move_y.astype(jnp.float32)
     angle_x = step * (move_x * (lane - BOX // 2).astype(jnp.float32))
     cos_x, sin_x = jnp.cos(angle_x), jnp.sin(angle_x)
     for row in range(freq // BOX):
@@ -37,10 +42,10 @@
 
 def kernel(
     n_cls, n_img, chunk, pieces,
-    ids_s, part_ref, cls_ref, ctf_ref, nw_ref, shift_ref,
+    ids_s, shift_ref, part_hbm, cls_hbm, ctf_hbm, nw_hbm,
     resp_ref, avg_ref,
-    wbuf, sel, onehot, cos_ref, sin_ref, temps, scores, rho_low, stat, mass_buf, send_buf, recv_buf, own,
-    right_sem, left_sem, gr_sem, ss_sem, sr_sem, ms_sem, mr_sem, ns_sem, nr_sem,
+    part_ref, cls_ref, ctf_ref, nw_ref, wbuf, sel, onehot, cos_ref, sin_ref, temps, scores, rho_low, stat, mass_buf, send_buf, recv_buf, own,
+    in_sem, right_sem, left_sem, gr_sem, ss_sem, sr_sem, ms_sem, mr_sem, ns_sem, nr_sem,
 ):
     rows = part_ref.shape[0]
     freq = ctf_ref.shape[1]
@@ -61,6 +66,17 @@
         pl.semaphore_signal(
             barrier, inc=1, device_id={"img": lax.rem(my_img + d, n_img)}, device_id_type=MESH
         )
+
+    inputs = [
+        pltpu.make_async_copy(src, dst, in_sem.at[i])
+        for i, (src, dst) in enumerate(
+            ((ctf_hbm, ctf_ref), (nw_hbm, nw_ref), (part_hbm, part_ref), (cls_hbm, cls_ref))
+        )
+    ]
+    for copy in inputs:
+        copy.start()
+    for copy in inputs[:3]:
+        copy.wait()
 
     for i in range(rows):
         sel[pl.ds(i, 1), :] = ctf_ref[pl.ds(ids_s[i], 1), :] * nw_ref[...]
@@ -119,7 +135,9 @@
         start_right(my_cls, p)
         start_left(my_cls, p)
 
-    fill_phase_tables(shift_ref[...], cos_ref, sin_ref)
+    fill_phase_tables(shift_ref, cos_ref, sin_ref)
+
+    inputs[3].wait()
 
     def build(c, power):
         at = pl.multiple_of(c * chunk, LANES)
@@ -152,21 +170,15 @@
 
     lax.fori_loop(1, n_cls - 1, relay_all, 0)
 
-    steps = width // (2 * chunk)
-
-    def cross(c, carry):
-        at = pl.multiple_of(c * 2 * chunk, LANES)
+    for p in range(pieces):
+        relay(n_cls - 1, p)
+        cols = slice(p * width, (p + 1) * width)
         scores[...] += lax.dot_general(
-            temps[:, pl.ds(at, 2 * chunk)],
-            wbuf[:, :, pl.ds(at, 2 * chunk)].reshape(total, 2 * chunk),
+            temps[:, cols],
+            wbuf[:, :, cols].reshape(total, width),
             NT,
             preferred_element_type=jnp.float32,
         )
-        return carry
-
-    for p in range(pieces):
-        relay(n_cls - 1, p)
-        lax.fori_loop(p * steps, (p + 1) * steps, cross, 0)
 
     marks = wbuf[:, :, 2 * freq :].reshape(total, pad_groups)[:, :groups].astype(jnp.float32)
     penalty = lax.dot_general(
@@ -252,13 +264,18 @@
 
         lax.fori_loop(0, part_freq // chunk, step, 0)
 
-    for d in range(1, n_img):
-        def store_peer(at, re, im, d=d):
+    def send_numer(t, carry):
+        d = 1 + lax.rem(t + 1, n_img - 1)
+
+        def store_peer(at, re, im):
             send_buf[d, :classes, pl.ds(at, chunk)] = re.astype(send_buf.dtype)
             send_buf[d, classes:, pl.ds(at, chunk)] = im.astype(send_buf.dtype)
 
         numer(lax.rem(my_img + d, n_img), store_peer)
         to_img(send_buf, recv_buf, d, ns_sem, nr_sem).start()
+        return carry
+
+    lax.fori_loop(0, n_img - 1, send_numer, 0)
 
     def store_own(at, re, im):
         own[:classes, pl.ds(at, chunk)] = re
@@ -326,9 +343,14 @@
             jax.ShapeDtypeStruct((cls_rows, total), jnp.float32),
             jax.ShapeDtypeStruct((2, cls_rows, part_freq), jnp.float32),
         ),
-        in_specs=[pl.BlockSpec(memory_space=pltpu.SMEM)] + [vmem] * 5,
+        in_specs=[pl.BlockSpec(memory_space=pltpu.SMEM)] * 2
+        + [pl.BlockSpec(memory_space=pl.ANY)] * 4,
         out_specs=(vmem, vmem),
         scratch_shapes=[
+            pltpu.VMEM((rows, 2 * freq), jnp.bfloat16),
+            pltpu.VMEM((cls_rows, 2 * freq), jnp.bfloat16),
+            pltpu.VMEM((groups, freq), jnp.float32),
+            pltpu.VMEM((1, freq), jnp.float32),
             pltpu.VMEM((n_cls, rows, 2 * freq + pad_groups), jnp.bfloat16),
             pltpu.VMEM((rows, freq), jnp.float32),
             pltpu.VMEM((rows, pad_groups), jnp.float32),
@@ -342,6 +364,7 @@
             pltpu.VMEM((n_img, 2 * cls_rows, part_freq), jnp.bfloat16),
             pltpu.VMEM((n_img, 2 * cls_rows, part_freq), jnp.bfloat16),
             pltpu.VMEM((2 * cls_rows, part_freq), jnp.float32),
+            dma((4,)),
             dma((n_cls, pieces)), dma((n_cls, pieces)), dma((n_cls, pieces)),
             dma((n_cls,)), dma((n_cls,)),
             dma((n_img,)), dma((n_img,)), dma((n_img,)), dma((n_img,)),
@@ -351,11 +374,11 @@
         ),
     )(
         group_ids,
+        shifts.T,
         particles.reshape(rows, 2 * freq),
         classes.reshape(cls_rows, 2 * freq),
         ctf,
-        noise_weight[None, :],
-        shifts,
+        noise_weight.reshape(1, freq),
     )
     return resp.T, avg.transpose(1, 0, 2)
 

time: 54.7 us -> 51.6 us (0.943)
  Pallas kernels: 44.1 us -> 42.3 us
  local copies, waits for them, and re-layouts: 9.56 us -> 8.21 us
    pallas_call x1, Pallas kernels: 44.1 us -> 42.3 us  [local(): pl.pallas_call(functools.partial(kernel, n_cls, n_img, chunk, pieces), ou...]
    unnamed x5 -> x4, local copies, waits for them, and re-layouts: 8.22 us -> 6.87 us
    reshape x0 -> x1, local copies, waits for them, and re-layouts: none -> 1.34 us  [local(): noise_weight.reshape(1, freq)]
    broadcast_in_dim x1 -> x0, local copies, waits for them, and re-layouts: 1.34 us -> none  [local(): noise_weight[None, :]]
where the time goes in v3:
time: 51.6 us; the launch traced here: 51.2 us
  Pallas kernels  42.3 us (82%)
  local copies, waits for them, and re-layouts  8.21 us (16%)
  between operations  0.64 us (1%)
    pallas_call x1, Pallas kernels, local(): pl.pallas_call(functools.partial(kernel, n_cls, n_img, chunk, pieces), ou...  42.3 us
    unnamed x4, local copies, waits for them, and re-layouts  6.87 us
    reshape x1, local copies, waits for them, and re-layouts, local(): noise_weight.reshape(1, freq)  1.34 us

profile of v3, /device:TPU:1, one launch (start us, length us, event | category | flops | bytes accessed | tf_op | source)
XLA Modules:
  0.0 51.2 jit_solution(540822066679095544)
XLA Ops:
  0.6 1.3 %reshape.15.nw_hbm = f32[1,4608]{1,0:T(1,128)} reshape(f32[4608]{0:T(1024)} %param.9) | data formatting | bytes 36864 | tf_op jit(solution)/shard_map/reshape | solution.py:381
  2.0 1.7 %copy.9 = bf16[2,8,2,4608]{3,1,2,0:T(8,128)(2,1)} copy(bf16[2,8,2,4608]{3,2,1,0:T(2,128)(2,1)} %bitcast.10) | data formatting | bytes 589824
  3.7 1.9 %copy.10 = bf16[4,8,2,4608]{3,1,2,0:T(8,128)(2,1)} copy(bf16[4,8,2,4608]{3,2,1,0:T(2,128)(2,1)} %bitcast.9) | data formatting | bytes 1179648
  5.6 42.3 %shard_map.77 = (f32[32,64]{1,0:T(8,128)}, f32[2,32,1152]{2,1,0:T(8,128)}) custom-call(s32[16]{0:T(128)} %ids_s.1, s32[2,24]{1,0:T(2,128)} %bitcast.13, bf16[16,9216]{1,0:T(8,128)(2,1)} %bitcast.8, bf16[32,9216]{1,0:T(8,128)(2,1)} %bitcast.7, f32[64,4608]{1,0:T(8,128)} %ctf_hbm.1, f32[1,4608]{1,0:T(1,128)} %reshape.15.nw_hbm), custom_call_target="tpu_custom_call" | custom-call | tf_op jit(solution)/shard_map/pallas_call | solution.py:340
  48.0 1.9 %copy.8 = f32[32,2,1152]{2,1,0:T(2,128)} copy(f32[32,2,1152]{2,0,1:T(8,128)} %bitcast.11) | data formatting | bytes 589824
  49.9 1.3 %copy.12 = f32[64,32]{0,1:T(8,128)} copy(f32[64,32]{0,1:T(8,128)} %bitcast.12) | data formatting | bytes 16384

commit v4 on v3

--- a/solution.py
+++ b/solution.py
@@ -70,7 +70,7 @@
     inputs = [
         pltpu.make_async_copy(src, dst, in_sem.at[i])
         for i, (src, dst) in enumerate(
-            ((ctf_hbm, ctf_ref), (nw_hbm, nw_ref), (part_hbm, part_ref), (cls_hbm, cls_ref))
+            ((ctf_hbm, ctf_ref), (nw_hbm, nw_ref.at[0]), (part_hbm, part_ref), (cls_hbm, cls_ref))
         )
     ]
     for copy in inputs:
@@ -86,7 +86,7 @@
     for part in range(2):
         cols = slice(part * freq, (part + 1) * freq)
         wbuf[my_cls, :, cols] = (
-            part_ref[:, cols].astype(jnp.float32) * sel[...]
+            part_ref[:, part].astype(jnp.float32) * sel[...]
         ).astype(jnp.bfloat16)
     pad_groups = wbuf.shape[2] - 2 * freq
     wbuf[my_cls, :, 2 * freq :] = onehot[...].astype(jnp.bfloat16)
@@ -142,8 +142,8 @@
     def build(c, power):
         at = pl.multiple_of(c * chunk, LANES)
         at_im = pl.multiple_of(freq + c * chunk, LANES)
-        re = cls_ref[:, pl.ds(at, chunk)].astype(jnp.float32)
-        im = cls_ref[:, pl.ds(at_im, chunk)].astype(jnp.float32)
+        re = cls_ref[:, 0, pl.ds(at, chunk)].astype(jnp.float32)
+        im = cls_ref[:, 1, pl.ds(at, chunk)].astype(jnp.float32)
         for r in range(poses):
             cos_r = cos_ref[r : r + 1, pl.ds(at, chunk)]
             sin_r = sin_ref[r : r + 1, pl.ds(at, chunk)]
@@ -302,7 +302,7 @@
         value_sum = own[at]
         for d in range(1, n_img):
             value_sum += recv_buf[d, at].astype(jnp.float32)
-        avg_ref[part] = value_sum / denom
+        avg_ref[:, part] = value_sum / denom
 
     for d in range(1, n_cls):
         stat_copy(d).wait_send()
@@ -341,14 +341,14 @@
         functools.partial(kernel, n_cls, n_img, chunk, pieces),
         out_shape=(
             jax.ShapeDtypeStruct((cls_rows, total), jnp.float32),
-            jax.ShapeDtypeStruct((2, cls_rows, part_freq), jnp.float32),
+            jax.ShapeDtypeStruct((cls_rows, 2, part_freq), jnp.float32),
         ),
         in_specs=[pl.BlockSpec(memory_space=pltpu.SMEM)] * 2
         + [pl.BlockSpec(memory_space=pl.ANY)] * 4,
         out_specs=(vmem, vmem),
         scratch_shapes=[
-            pltpu.VMEM((rows, 2 * freq), jnp.bfloat16),
-            pltpu.VMEM((cls_rows, 2 * freq), jnp.bfloat16),
+            pltpu.VMEM((rows, 2, freq), jnp.bfloat16),
+            pltpu.VMEM((cls_rows, 2, freq), jnp.bfloat16),
             pltpu.VMEM((groups, freq), jnp.float32),
             pltpu.VMEM((1, freq), jnp.float32),
             pltpu.VMEM((n_cls, rows, 2 * freq + pad_groups), jnp.bfloat16),
@@ -375,12 +375,12 @@
     )(
         group_ids,
         shifts.T,
-        particles.reshape(rows, 2 * freq),
-        classes.reshape(cls_rows, 2 * freq),
+        particles,
+        classes,
         ctf,
-        noise_weight.reshape(1, freq),
-    )
-    return resp.T, avg.transpose(1, 0, 2)
+        noise_weight,
+    )
+    return resp.T, avg
 
 
 def solution(mesh):

time: 51.6 us -> 47.5 us (0.921)
  local copies, waits for them, and re-layouts: 8.21 us -> 3.03 us
  Pallas kernels: 42.3 us -> 43.6 us
    unnamed x4 -> x2, local copies, waits for them, and re-layouts: 6.87 us -> 3.03 us
    reshape x1 -> x0, local copies, waits for them, and re-layouts: 1.34 us -> none  [local(): noise_weight.reshape(1, freq)]
    pallas_call x1, Pallas kernels: 42.3 us -> 43.6 us  [local(): pl.pallas_call(functools.partial(kernel, n_cls, n_img, chunk, pieces), ou...]
where the time goes in v4:
time: 47.5 us; the launch traced here: 47.2 us
  Pallas kernels  43.6 us (92%)
  local copies, waits for them, and re-layouts  3.03 us (6%)
  between operations  0.64 us (1%)
    pallas_call x1, Pallas kernels, local(): pl.pallas_call(functools.partial(kernel, n_cls, n_img, chunk, pieces), ou...  43.6 us
    unnamed x2, local copies, waits for them, and re-layouts  3.03 us

profile of v4, /device:TPU:1, one launch (start us, length us, event | category | flops | bytes accessed | tf_op | source)
XLA Modules:
  0.0 47.2 jit_solution(1772385437524607502)
XLA Ops:
  0.6 43.6 %shard_map.77 = (f32[32,64]{1,0:T(8,128)}, f32[32,2,1152]{2,1,0:T(2,128)}) custom-call(s32[16]{0:T(128)} %ids_s.1, s32[2,24]{1,0:T(2,128)} %bitcast.3, bf16[16,2,4608]{2,1,0:T(2,128)(2,1)} %part_hbm.1, bf16[32,2,4608]{2,1,0:T(2,128)(2,1)} %cls_hbm.1, f32[64,4608]{1,0:T(8,128)} %ctf_hbm.1, f32[4608]{0:T(1024)} %nw_hbm.1), custom_call_target="tpu_custom_call" | custom-call | tf_op jit(solution)/shard_map/pallas_call | solution.py:340
  44.2 1.3 %copy.10 = f32[64,32]{0,1:T(8,128)} copy(f32[64,32]{0,1:T(8,128)} %bitcast.2) | data formatting | bytes 16384
  45.5 1.7 %copy.11 = f32[32,2,1152]{2,1,0:T(2,128)} copy(f32[32,2,1152]{2,1,0:T(2,128)} %get-tuple-element.9) | data formatting | bytes 589824

commit v5 on v4

--- a/solution.py
+++ b/solution.py
@@ -157,18 +157,19 @@
             preferred_element_type=jnp.float32,
         )
 
-    power = lax.fori_loop(
-        0, freq // chunk, build, jnp.zeros((classes, groups), jnp.float32)
-    )
-
-    scores[...] = jnp.zeros_like(scores)
-
     def relay_all(h, carry):
         for p in range(pieces):
             relay(h, p)
         return carry
 
-    lax.fori_loop(1, n_cls - 1, relay_all, 0)
+    steps = freq // chunk
+    early = steps * 2 // 3
+    power = lax.fori_loop(0, early, build, jnp.zeros((classes, groups), jnp.float32))
+    if n_cls > 2:
+        relay_all(1, 0)
+    power = lax.fori_loop(early, steps, build, power)
+    scores[...] = jnp.zeros_like(scores)
+    lax.fori_loop(2, n_cls - 1, relay_all, 0)
 
     for p in range(pieces):
         relay(n_cls - 1, p)

time: 47.5 us -> 45.8 us (0.964)
  Pallas kernels: 43.6 us -> 41.9 us
    pallas_call x1, Pallas kernels: 43.6 us -> 41.9 us  [local(): pl.pallas_call(functools.partial(kernel, n_cls, n_img, chunk, pieces), ou...]
where the time goes in v5:
time: 45.8 us; the launch traced here: 45.5 us
  Pallas kernels  41.9 us (91%)
  local copies, waits for them, and re-layouts  3.03 us (7%)
  between operations  0.64 us (1%)
    pallas_call x1, Pallas kernels, local(): pl.pallas_call(functools.partial(kernel, n_cls, n_img, chunk, pieces), ou...  41.9 us
    unnamed x2, local copies, waits for them, and re-layouts  3.03 us

profile of v5, /device:TPU:1, one launch (start us, length us, event | category | flops | bytes accessed | tf_op | source)
XLA Modules:
  0.0 45.5 jit_solution(1688667514689563490)
XLA Ops:
  0.6 41.9 %shard_map.77 = (f32[32,64]{1,0:T(8,128)}, f32[32,2,1152]{2,1,0:T(2,128)}) custom-call(s32[16]{0:T(128)} %ids_s.1, s32[2,24]{1,0:T(2,128)} %bitcast.3, bf16[16,2,4608]{2,1,0:T(2,128)(2,1)} %part_hbm.1, bf16[32,2,4608]{2,1,0:T(2,128)(2,1)} %cls_hbm.1, f32[64,4608]{1,0:T(8,128)} %ctf_hbm.1, f32[4608]{0:T(1024)} %nw_hbm.1), custom_call_target="tpu_custom_call" | custom-call | tf_op jit(solution)/shard_map/pallas_call | solution.py:341
  42.5 1.3 %copy.10 = f32[64,32]{0,1:T(8,128)} copy(f32[64,32]{0,1:T(8,128)} %bitcast.2) | data formatting | bytes 16384
  43.8 1.7 %copy.11 = f32[32,2,1152]{2,1,0:T(2,128)} copy(f32[32,2,1152]{2,1,0:T(2,128)} %get-tuple-element.9) | data formatting | bytes 589824
